TPU v7x, 256 devices: a whole 4x4x8 slice. The times are simulated.
256 devices in a mesh: frame: 4 (over x), space: 64 (over z, y, core).
Axes of the slice: x: 4, y: 4, z: 8, core: 2. Of those that a mesh axis runs over, the one named last changes fastest.
Arguments:
- queries: bfloat16 [32768, 3072], P(('frame', 'space')), as said below
- keys: bfloat16 [32768, 3072], P(('frame', 'space')), as said below
- values: bfloat16 [32768, 3072], P(('frame', 'space')), may hold values from -5 to 5
- level_weight: float32 [3, 24, 32768], P(None, None, ('frame', 'space')), may hold values from 0.2 to 2
- frame_len: int32 [256, 4], P(('frame', 'space')), may hold values from 1 to 53, 128 in all within a row
- window_back: int32 [256, 4], P(('frame', 'space')), may hold values from 2 to 63
Outputs:
- mixed: bfloat16 [32768, 3072], P(('frame', 'space'))
Inputs may be any that keep to these rules, and one draw needn't show every extreme that they name: `queries`: entries up to 60 in magnitude. `keys`: entries up to 4 in magnitude. `frame_len`: each row is the frame lengths of one device's 128 tokens, summing to 128; the longest frame of each row has exactly 53 tokens.
All inputs are finite; a program needn't handle non-finite values.
Results may differ from a plain program's by a relative error of at most 0.0085.
Values may be sent and summed in bfloat16 or wider, within the bound.
A program may use at most 64 MiB of HBM per device.

v0:
```python
import math
import jax
import jax.numpy as jnp
from jax import lax
from jax.sharding import PartitionSpec as P

HEADS = 24
HEAD_DIM = 128
EPSILON = 1e-06


def unit_rows(matrix):
    return (matrix * lax.rsqrt(jnp.mean(matrix * matrix, -1, keepdims=True) + EPSILON)).astype(
        jnp.bfloat16
    )


def visible_mask(lengths, backward, count):
    starts = jnp.cumsum(lengths) - lengths
    lowest = jnp.maximum(starts - backward, 0)
    position = jnp.arange(count, dtype=jnp.int32)
    inside = (position[:, None] >= starts[None, :]).astype(jnp.int32)
    frame_of = jnp.sum(inside, 1) - 1
    onehot = frame_of[:, None] == jnp.arange(lengths.shape[0], dtype=jnp.int32)[None, :]
    floor_row = jnp.sum(jnp.where(onehot, lowest[None, :], 0), 1)
    return (position[None, :] <= position[:, None]) & (position[None, :] >= floor_row[:, None])


def causal_mix(query_heads, key_heads, value_heads, visible, heads, head_dim):
    pieces = []
    for first_head in range(0, heads, 4):
        query_part = query_heads[:, first_head : first_head + 4]
        key_part = key_heads[:, first_head : first_head + 4]
        value_part = value_heads[:, first_head : first_head + 4]
        scores = jnp.einsum(
            "thd,shd->hts", query_part, key_part, preferred_element_type=jnp.float32
        ) / math.sqrt(head_dim)
        scores = jnp.where(visible[None], scores, -jnp.inf)
        row_max = jnp.max(scores, -1, keepdims=True)
        weights = jnp.exp(scores - row_max)
        totals = jnp.sum(weights, -1)
        mixed_part = jnp.einsum(
            "hts,shd->thd",
            weights.astype(jnp.bfloat16),
            value_part,
            preferred_element_type=jnp.float32,
        )
        pieces.append(mixed_part / jnp.transpose(totals)[:, :, None])
    return jnp.concatenate(pieces, 1)


def body(queries, keys, values, level_weight, frame_len, window_back):
    tok_rows = queries.shape[0]
    frames_total = lax.axis_size("frame")
    frame_pos = lax.axis_index("frame")
    space_count = lax.axis_size("space")
    query_heads = queries.reshape(tok_rows, HEADS, HEAD_DIM)
    key_heads = keys.reshape(tok_rows, HEADS, HEAD_DIM)
    value_heads = values.reshape(tok_rows, HEADS, HEAD_DIM)
    normal_k = unit_rows(key_heads.astype(jnp.float32))
    local_state = jnp.einsum(
        "thd,the->hde", normal_k, value_heads, preferred_element_type=jnp.float32
    )
    state_rows = local_state.reshape(HEADS * HEAD_DIM, HEAD_DIM)
    block_part = lax.psum(state_rows, "space")
    tree_depth = frames_total.bit_length() - 1
    levels = []
    all_blocks = lax.all_gather(
        block_part[None].astype(jnp.bfloat16), "frame", axis=0, tiled=True
    ).astype(jnp.float32)
    block_ids = jnp.arange(frames_total, dtype=jnp.int32)
    for bit_index in range(tree_depth):
        start_block = frame_pos // 2 ** (bit_index + 1) * 2 ** (bit_index + 1)
        bit_set = frame_pos // 2**bit_index % 2
        inside = (
            (block_ids >= start_block) & (block_ids < start_block + 2**bit_index) & (bit_set == 1)
        )
        levels.append(jnp.sum(jnp.where(inside[:, None, None], all_blocks, 0.0), 0))
    level_rows = jnp.stack(levels).astype(jnp.bfloat16)
    level_heads = level_rows.reshape(tree_depth, HEADS, HEAD_DIM, HEAD_DIM)
    visible = visible_mask(frame_len[0], window_back[0], tok_rows)
    local_mix = causal_mix(query_heads, key_heads, value_heads, visible, HEADS, HEAD_DIM)
    result = local_mix * jnp.transpose(level_weight[0])[:, :, None]
    normal_q = unit_rows(query_heads.astype(jnp.float32))
    level_reads = jnp.einsum(
        "thd,lhde->lthe", normal_q, level_heads, preferred_element_type=jnp.float32
    )
    block_tokens = tok_rows * space_count
    for level_index in range(tree_depth):
        level_scale = 1.0 / math.sqrt(HEAD_DIM * 2**level_index * block_tokens)
        result = result + jnp.transpose(level_weight[1 + level_index])[:, :, None] * (
            level_scale * level_reads[level_index]
        )
    return result.reshape(tok_rows, HEADS * HEAD_DIM).astype(jnp.bfloat16)


def solution(mesh):
    return jax.shard_map(
        body,
        mesh=mesh,
        in_specs=(
            P(("frame", "space"), None),
            P(("frame", "space"), None),
            P(("frame", "space"), None),
            P(None, None, ("frame", "space")),
            P(("frame", "space"), None),
            P(("frame", "space"), None),
        ),
        out_specs=P(("frame", "space"), None),
        check_vma=False,
    )
```

profile of v0, /device:TPU:1, one launch (start us, length us, event | category | flops | bytes accessed | tf_op | source)
XLA Modules:
  0.0 333.2 jit_solution(7249709284273984305)
XLA Ops:
  6.5 1.6 copy.53
  8.1 0.4 copy.55
  8.7 0.7 fusion.32
  9.4 264.9 %all-reduce.1 = bf16[3072,128]{1,0:T(8,128)(2,1)} all-reduce(f32[3072,128]{1,0:T(8,128)S(1)} %bitcast.114), channel_id=1, replica_groups=mesh['frame'=4,'space'=64] {'space'}, use_global_device_ids=true, to_apply=%region_16.17 | all-reduce | flops 393216 | bytes 2359296 | tf_op jit(solution)/shard_map/psum | solution.py:65
  274.8 1.2 copy.51
  276.0 1.2 fusion.75
  277.3 1.2 fusion.76
  278.6 1.2 fusion.77
  279.9 1.2 fusion.78
  281.2 1.2 fusion.79
  282.5 1.2 fusion.80
  285.1 1.6 copy.78
  287.1 29.0 %all-gather.3.cloned.1.call-done = bf16[12288,128]{1,0:T(8,128)(2,1)} async-done(((bf16[3072,128]{1,0:T(8,128)(2,1)}), bf16[12288,128]{1,0:T(8,128)(2,1)}) %all-gather.3.cloned.1.call-update) | async-done | bytes 3145744 | tf_op jit(solution)/shard_map/all_gather | solution.py:68
  316.1 3.1 fusion
  319.2 0.4 copy.73
  319.6 0.4 copy.74
  320.0 0.6 convolution_bitcast_fusion
  320.7 1.6 copy.77
  322.4 0.5 copy.80
  322.9 0.5 mul.97
  323.3 0.5 mul.104
  323.8 0.4 copy-done.2
  324.3 0.5 copy-done.3
  324.7 1.6 fusion.7
  (46 shorter events, 2.8 us)
Async XLA Ops:
  6.5 1.6 copy-start.4
  6.5 309.5 %all-gather.3.cloned.1.call-start = ((), (), s32[]{:S(2)}) async-start(), calls=%async_computation | async-start | bytes 3932160 | tf_op jit(solution)/shard_map/all_gather | solution.py:68
  8.1 1.3 copy-start.1
  9.4 265.0 %copy-start.7 = (s32[1,4]{1,0:T(1,128)S(1)}, s32[1,4]{1,0:T(1,128)}, u32[]{:S(2)}) copy-start(s32[1,4]{1,0:T(1,128)} %param.10) | copy-start | bytes 52
  9.4 265.2 %copy-start.8 = (s32[1,4]{1,0:T(1,128)S(1)}, s32[1,4]{1,0:T(1,128)}, u32[]{:S(2)}) copy-start(s32[1,4]{1,0:T(1,128)} %param.11) | copy-start | bytes 52
  9.4 265.4 %copy-start.5 = (bf16[128,3072]{1,0:T(8,128)(2,1)S(1)}, bf16[128,3072]{1,0:T(8,128)(2,1)}, u32[]{:S(2)}) copy-start(bf16[128,3072]{1,0:T(8,128)(2,1)} %param.6) | copy-start | bytes 2359300
  279.9 3.9 %copy-start.6 = (f32[3,24,128]{2,1,0:T(8,128)S(1)}, f32[3,24,128]{2,1,0:T(8,128)}, u32[]{:S(2)}) copy-start(f32[3,24,128]{2,1,0:T(8,128)} %param.9) | copy-start | bytes 110596
  285.1 1.8 copy-start
  322.8 1.4 copy-start.2
  322.9 1.9 copy-start.3
Sparse Core Ops, SparseCore 0:
  274.5 41.5 all-gather.2
where the time goes:
time: 333 us
  blocking collectives  265 us (80%)
  waiting for transfers between devices  29 us (9%)
  between operations  13.7 us (4%)
  local copies, waits for them, and re-layouts  9.88 us (3%)
  matrix products  9.67 us (3%)
  other arithmetic  6 us (2%)
    psum x1, blocking collectives, body(): block_part = lax.psum(state_rows, 'space')  265 us
    all_gather x1, waiting for transfers between devices, body(): lax.all_gather(block_part[None].astype(jnp.bfloat16), 'frame', axis=0, ti...  29 us
    dot_general x6, matrix products, causal_mix(): jnp.einsum('thd,shd->hts', query_part, key_part, preferred_element_type=j...  7.32 us
  transfers between devices with their start and end apart: 1, of which 1 were waited for; matrix products, arithmetic and copies ran while one was open for 4% of the time, Pallas kernels for 0%

commit v1 on v0

--- a/solution.py
+++ b/solution.py
@@ -65,8 +65,14 @@
     block_part = lax.psum(state_rows, "space")
     tree_depth = frames_total.bit_length() - 1
     levels = []
-    all_blocks = lax.all_gather(
-        block_part[None].astype(jnp.bfloat16), "frame", axis=0, tiled=True
+    all_blocks = jnp.concatenate(
+        lax.all_to_all(
+            jnp.stack([block_part[None].astype(jnp.bfloat16)] * lax.axis_size("frame")),
+            "frame",
+            0,
+            0,
+        ),
+        axis=0,
     ).astype(jnp.float32)
     block_ids = jnp.arange(frames_total, dtype=jnp.int32)
     for bit_index in range(tree_depth):

time: 333 us -> 321 us (0.964); the launches traced: 333 us -> 316 us
  waiting for transfers between devices: 29 us -> 8.85 us
  between operations: 13.7 us -> 0.37 us
  other arithmetic: 6 us -> 12.6 us
  local copies, waits for them, and re-layouts: 9.88 us -> 16.3 us
  starting transfers between devices: 0.01 us -> 4.01 us
    all_gather x1 -> x0, waiting for transfers between devices: 29 us -> none  [body(): lax.all_gather(block_part[None].astype(jnp.bfloat16), 'frame', axis=0, ti...]
    all_to_all x0 -> x1, waiting for transfers between devices: none -> 8.85 us  [body(): lax.all_to_all(jnp.stack([block_part[None].astype(jnp.bfloat16)] * lax.ax...]
    reduce_sum x6, other arithmetic: 0.37 us -> 5.24 us  [causal_mix(): totals = jnp.sum(weights, -1)]
    all_to_all x0 -> x1, starting transfers between devices: none -> 4.01 us  [body(): lax.all_to_all(jnp.stack([block_part[None].astype(jnp.bfloat16)] * lax.ax...]
  transfers between devices with their start and end apart: 1 -> 1, of which waited for: 1 -> 1; matrix products, arithmetic and copies ran while one was open for 4% -> 7% of each run, Pallas kernels for 0% -> 0%
where the time goes in v1:
time: 321 us; the launch traced here: 316 us
  blocking collectives  264 us (82%)
  local copies, waits for them, and re-layouts  16.3 us (5%)
  other arithmetic  12.6 us (4%)
  matrix products  9.34 us (3%)
  waiting for transfers between devices  8.85 us (3%)
  starting transfers between devices  4.01 us (1%)
    psum x1, blocking collectives, body(): block_part = lax.psum(state_rows, 'space')  264 us
    all_to_all x1, waiting for transfers between devices, body(): lax.all_to_all(jnp.stack([block_part[None].astype(jnp.bfloat16)] * lax.ax...  8.85 us
    dot_general x6, matrix products, causal_mix(): jnp.einsum('thd,shd->hts', query_part, key_part, preferred_element_type=j...  7 us
  transfers between devices with their start and end apart: 1, of which 1 were waited for; matrix products, arithmetic and copies ran while one was open for 7% of the time, Pallas kernels for 0%

profile of v1, /device:TPU:1, one launch (start us, length us, event | category | flops | bytes accessed | tf_op | source)
XLA Modules:
  0.0 315.8 jit_solution(2419693226612850592)
XLA Ops:
  0.0 1.6 copy.83
  2.2 0.7 fusion.32
  2.9 264.3 %all-reduce.1 = bf16[3072,128]{1,0:T(8,128)(2,1)S(1)} all-reduce(f32[3072,128]{1,0:T(8,128)S(1)} %bitcast.116), channel_id=1, replica_groups=mesh['frame'=4,'space'=64] {'space'}, use_global_device_ids=true, to_apply=%region_16.17 | all-reduce | flops 393216 | bytes 2359296 | tf_op jit(solution)/shard_map/psum | solution.py:65
  267.1 2.1 stack.16
  269.2 4.0 %all-to-all-start = ((bf16[4,1,3072,128]{3,2,1,0:T(8,128)(2,1)}), bf16[4,1,3072,128]{3,2,1,0:T(8,128)(2,1)S(1)}, u32[]{:S(2)}, u32[]{:S(2)}) async-start(bf16[4,1,3072,128]{3,2,1,0:T(8,128)(2,1)} %stack.16), calls=%async_computation | async-start | bytes 6291456 | tf_op jit(solution)/shard_map/all_to_all | solution.py:69
  273.2 2.3 copy.81
  276.0 2.0 fusion.75
  278.0 1.9 fusion.76
  279.9 0.9 fusion.77
  280.8 0.9 fusion.78
  281.8 0.9 fusion.79
  283.1 1.1 fusion.36
  284.2 1.0 fusion.38
  285.2 1.0 fusion.40
  286.2 1.0 fusion.42
  287.2 1.1 fusion.44
  290.1 1.4 broadcast_multiply_fusion
  291.5 3.0 copy.108
  294.7 1.3 fusion.4
  296.0 8.8 %all-to-all-done = bf16[4,1,3072,128]{3,2,1,0:T(8,128)(2,1)S(1)} async-done(((bf16[4,1,3072,128]{3,2,1,0:T(8,128)(2,1)}), bf16[4,1,3072,128]{3,2,1,0:T(8,128)(2,1)S(1)}, u32[]{:S(2)}, u32[]{:S(2)}) %all-to-all-start) | async-done | bytes 3145760 | tf_op jit(solution)/shard_map/all_to_all | solution.py:69
  304.9 2.5 fusion
  307.4 1.6 copy.103
  310.2 1.6 copy.107
  314.2 1.6 fusion.7
  (64 shorter events, 6.7 us)
Async XLA Ops:
  0.0 1.6 copy-start.9
  1.6 1.3 copy-start.2
  2.0 0.9 copy-start.7
  269.2 35.6 %all-to-all-start = ((bf16[4,1,3072,128]{3,2,1,0:T(8,128)(2,1)}), bf16[4,1,3072,128]{3,2,1,0:T(8,128)(2,1)S(1)}, u32[]{:S(2)}, u32[]{:S(2)}) async-start(bf16[4,1,3072,128]{3,2,1,0:T(8,128)(2,1)} %stack.16), calls=%async_computation | async-start | bytes 6291456 | tf_op jit(solution)/shard_map/all_to_all | solution.py:69
  273.2 2.3 copy-start.16
  273.2 2.5 copy-start.17
  275.7 4.1 %copy-start = (bf16[128,3072]{0,1:T(8,128)(2,1)S(1)}, bf16[128,3072]{0,1:T(8,128)(2,1)}, u32[]{:S(2)}) copy-start(bf16[128,3072]{0,1:T(8,128)(2,1)} %copy.81) | copy-start | bytes 2359300
  275.7 4.1 %copy-start.3 = (bf16[128,3072]{0,1:T(8,128)(2,1)S(1)}, bf16[128,3072]{0,1:T(8,128)(2,1)}, u32[]{:S(2)}) copy-start(bf16[128,3072]{0,1:T(8,128)(2,1)} %copy-done.2) | copy-start | bytes 2359300
  279.9 3.1 copy-start.15
  283.0 5.3 %copy-start.8 = (bf16[128,3072]{0,1:T(8,128)(2,1)S(1)}, bf16[128,3072]{0,1:T(8,128)(2,1)}, u32[]{:S(2)}) copy-start(bf16[128,3072]{0,1:T(8,128)(2,1)} %copy-done.7) | copy-start | bytes 2359300
  283.0 5.3 %copy-start.14 = (f32[4,128,128]{1,2,0:T(8,128)S(1)}, f32[4,128,128]{1,2,0:T(8,128)}, u32[]{:S(2)}) copy-start(f32[4,128,128]{1,2,0:T(8,128)} %get-tuple-element.15) | copy-start | bytes 786436
  283.0 5.5 %copy-start.13 = (f32[4,128,128]{1,2,0:T(8,128)S(1)}, f32[4,128,128]{1,2,0:T(8,128)}, u32[]{:S(2)}) copy-start(f32[4,128,128]{1,2,0:T(8,128)} %get-tuple-element.17) | copy-start | bytes 786436
  287.2 1.6 copy-start.12
  288.5 1.0 copy-start.11
  288.7 1.0 copy-start.10
  307.4 1.6 copy-start.6
  307.4 2.0 copy-start.1
  312.3 1.4 copy-start.4
  312.3 1.9 copy-start.5
